TPU v7x, 32 devices: a whole 2x2x4 slice. The times are simulated.
32 devices in a mesh: seq: 8 (over z, x), head: 4 (over y, core).
Axes of the slice: x: 2, y: 2, z: 4, core: 2. Of those that a mesh axis runs over, the one named last changes fastest.
Arguments:
- query: bfloat16 [1024, 16, 576], P('seq', 'head'), may hold values from -48 to 48
- latents: bfloat16 [1024, 576], P('seq'), may hold values from -6 to 6
- out_grad: bfloat16 [1024, 16, 512], P('seq', 'head'), may hold values from -6 to 6
- saved_out: bfloat16 [1024, 16, 512], P('seq', 'head'), may hold values from -6 to 6
- first_key: int32 [1024], P('seq'), may hold values from 0 to 1022, as said below
Outputs:
- query_grad: float32 [1024, 16, 576], P('seq', 'head')
- latent_grad: float32 [1024, 576], P(('seq', 'head'))
Inputs may be any that keep to these rules, and one draw needn't show every extreme that they name: first_key[i] <= i - 1 for i >= 1, first_key[0] = 0, and first_key[i] >= i - 512; the lower bound is met at the first position of every block of 128 from position 512 on.
All inputs are finite; a program needn't handle non-finite values.
Results may differ from a plain program's by a relative error of at most 0.0039.
Values may be sent and summed in bfloat16 or wider, within the bound.
A program may use at most 64 MiB of HBM per device.

v0:
```python
import jax
import jax.numpy as jnp
from jax import lax
from jax.sharding import PartitionSpec as P

VAL = 512
QK_HEAD = 192
STEPS = 5


def shifted(block, axis, distance):
    devices = range(lax.axis_size(axis))
    route = [(i - distance, i) for i in devices if i - distance in devices]
    return lax.ppermute(block, axis, route)


def visibility(first, query_start, key_start, rows, heads, keys):
    query_pos = jnp.repeat(query_start + jnp.arange(rows, dtype=jnp.int32), heads)
    first_rows = jnp.repeat(first, heads)
    key_pos = key_start + jnp.arange(keys, dtype=jnp.int32)
    return (key_pos[None, :] >= first_rows[:, None]) & (key_pos[None, :] <= query_pos[:, None])


def attention_grads(queries, window, grads_out, outputs, visible):
    softmax_scale = QK_HEAD ** (-0.5)
    scores = jnp.dot(queries, window.T, preferred_element_type=jnp.float32) * softmax_scale
    scores = jnp.where(visible, scores, -1e30)
    row_max = jnp.max(scores, axis=1, keepdims=True)
    row_total = jnp.sum(jnp.where(visible, jnp.exp(scores - row_max), 0.0), axis=1, keepdims=True)
    log_norm = row_max + jnp.log(row_total)
    probs = jnp.where(visible, jnp.exp(scores - log_norm), 0.0)
    row_dot = jnp.sum(
        grads_out.astype(jnp.float32) * outputs.astype(jnp.float32), axis=1, keepdims=True
    )
    prob_grad = jnp.dot(grads_out, window[:, :VAL].T, preferred_element_type=jnp.float32)
    score_grad = (probs * (prob_grad - row_dot)).astype(jnp.bfloat16)
    probs_low = probs.astype(jnp.bfloat16)
    query_grad = jnp.dot(score_grad, window, preferred_element_type=jnp.float32) * softmax_scale
    contract = (((0,), (0,)), ((), ()))
    latent_grad = (
        lax.dot_general(score_grad, queries, contract, preferred_element_type=jnp.float32)
        * softmax_scale
    )
    value_grad = lax.dot_general(probs_low, grads_out, contract, preferred_element_type=jnp.float32)
    padding = jnp.zeros((window.shape[0], window.shape[1] - VAL), jnp.float32)
    latent_grad = latent_grad + jnp.concatenate([value_grad, padding], axis=1)
    return (query_grad, latent_grad)


def body(query, latents, out_grad, saved_out, first_key):
    rows, heads, width = query.shape
    here = lax.axis_index("seq")
    blocks = [latents]
    current = latents
    for hop_index in range(STEPS - 1):
        current = shifted(current, "seq", 1)
        blocks.append(current)
    window = jnp.concatenate(blocks[::-1], axis=0)
    query_start = here * rows
    visible = visibility(
        first_key, query_start, query_start - (STEPS - 1) * rows, rows, heads, STEPS * rows
    )
    query_grad, latent_grad = attention_grads(
        query.reshape(rows * heads, width),
        window,
        out_grad.reshape(rows * heads, VAL),
        saved_out.reshape(rows * heads, VAL),
        visible,
    )
    pieces = latent_grad.reshape(STEPS, rows, width)
    carried = pieces[0]
    for hop_index in range(1, STEPS):
        carried = shifted(carried, "seq", -1) + pieces[hop_index]
    carried = lax.psum_scatter(carried, "head", scatter_dimension=0, tiled=True)
    return (query_grad.reshape(rows, heads, width), carried)


def solution(mesh):
    in_specs = (
        P("seq", "head", None),
        P("seq", None),
        P("seq", "head", None),
        P("seq", "head", None),
        P("seq"),
    )
    out_specs = (P("seq", "head", None), P(("seq", "head"), None))
    return jax.shard_map(body, mesh=mesh, in_specs=in_specs, out_specs=out_specs, check_vma=False)
```

profile of v0, /device:TPU:0, one launch (start us, length us, event | category | flops | bytes accessed | tf_op | source)
XLA Modules:
  0.0 114.5 jit_solution(516952720798494243)
XLA Ops:
  7.2 0.0 copy-start
  7.2 0.0 copy-start.3
  7.2 0.0 copy-start.1
  7.2 0.0 reduce-scatter.4.cloned.1.call-start
  7.2 5.0 %collective-permute-start = (bf16[128,576]{0,1:T(8,128)(2,1)}, bf16[128,576]{0,1:T(8,128)(2,1)S(1)}, u32[]{:S(2)}, u32[]{:S(2)}) collective-permute-start(bf16[128,576]{0,1:T(8,128)(2,1)} %param.6), channel_id=1, source_target_pairs={{0,4},{4,8},{8,12},{12,16},{16,20},{20,24},{24,28},{1,5},{5,9},{9,... | collective-permute-start | bytes 442376 | tf_op jit(solution)/shard_map/ppermute | solution.py:14
  12.3 3.4 %collective-permute-done = bf16[128,576]{0,1:T(8,128)(2,1)S(1)} collective-permute-done((bf16[128,576]{0,1:T(8,128)(2,1)}, bf16[128,576]{0,1:T(8,128)(2,1)S(1)}, u32[]{:S(2)}, u32[]{:S(2)}) %collective-permute-start) | collective-permute-done | bytes 147488 | tf_op jit(solution)/shard_map/ppermute | solution.py:14
  15.7 4.3 %collective-permute-start.1 = (bf16[128,576]{0,1:T(8,128)(2,1)S(1)}, bf16[128,576]{0,1:T(8,128)(2,1)S(1)}, u32[]{:S(2)}, u32[]{:S(2)}) collective-permute-start(bf16[128,576]{0,1:T(8,128)(2,1)S(1)} %collective-permute-done), channel_id=1, source_target_pairs={{0,4},{4,8},{8,12},{12,16},{16,20},{20,24},{24,28},{1,5},{5,9},{9,... | collective-permute-start | bytes 442376 | tf_op jit(solution)/shard_map/ppermute | solution.py:14
  19.9 2.6 %collective-permute-done.1 = bf16[128,576]{0,1:T(8,128)(2,1)S(1)} collective-permute-done((bf16[128,576]{0,1:T(8,128)(2,1)S(1)}, bf16[128,576]{0,1:T(8,128)(2,1)S(1)}, u32[]{:S(2)}, u32[]{:S(2)}) %collective-permute-start.1) | collective-permute-done | bytes 147488 | tf_op jit(solution)/shard_map/ppermute | solution.py:14
  22.6 4.4 %collective-permute-start.2 = (bf16[128,576]{0,1:T(8,128)(2,1)S(1)}, bf16[128,576]{0,1:T(8,128)(2,1)S(1)}, u32[]{:S(2)}, u32[]{:S(2)}) collective-permute-start(bf16[128,576]{0,1:T(8,128)(2,1)S(1)} %collective-permute-done.1), channel_id=1, source_target_pairs={{0,4},{4,8},{8,12},{12,16},{16,20},{20,24},{24,28},{1,5},{5,9},{9,... | collective-permute-start | bytes 442376 | tf_op jit(solution)/shard_map/ppermute | solution.py:14
  27.0 1.6 %multiply_reduce_fusion = f32[128,4]{1,0:T(8,128)S(1)} fusion(bf16[128,4,512]{2,1,0:T(4,128)(2,1)} %param.8, bf16[128,4,512]{2,1,0:T(4,128)(2,1)} %param.7), kind=kLoop, calls=%fused_computation.12 | loop fusion | flops 1048064 | bytes 1050624 | tf_op jit(solution)/shard_map/reduce_sum | solution.py:32
  28.6 1.0 collective-permute-done.2
  29.6 5.2 %collective-permute-start.3 = (bf16[128,576]{0,1:T(8,128)(2,1)S(1)}, bf16[128,576]{0,1:T(8,128)(2,1)S(1)}, u32[]{:S(2)}, u32[]{:S(2)}) collective-permute-start(bf16[128,576]{0,1:T(8,128)(2,1)S(1)} %collective-permute-done.2), channel_id=1, source_target_pairs={{0,4},{4,8},{8,12},{12,16},{16,20},{20,24},{24,28},{1,5},{5,9},{9,... | collective-permute-start | bytes 442376 | tf_op jit(solution)/shard_map/ppermute | solution.py:14
  34.9 0.0 copy-done
  34.9 0.1 reshape.44
  35.0 0.1 broadcast_in_dim.21
  35.1 0.1 le.6
  35.2 0.1 sub.37
  35.3 0.0 copy-done.3
  35.3 0.1 broadcast_in_dim.20
  35.4 0.1 ge.16
  35.5 0.0 copy-done.1
  35.5 0.8 copy.13
  36.3 0.0 copy-start.2
  36.3 0.3 reshape.43
  36.7 0.8 collective-permute-done.3
  37.7 0.0 copy-done.2
  37.7 0.8 fusion.12
  38.6 0.4 select_reduce_fusion
  39.0 0.8 fusion.6
  39.7 0.8 fusion.4
  40.6 0.7 pad_add_fusion
  41.3 1.3 %collective-permute-start.4 = (f32[128,576]{0,1:T(8,128)S(1)}, f32[128,576]{0,1:T(8,128)S(1)}, u32[]{:S(2)}, u32[]{:S(2)}) collective-permute-start(f32[128,576]{0,1:T(8,128)S(1)} %slice.30), channel_id=1, source_target_pairs={{4,0},{8,4},{12,8},{16,12},{20,16},{24,20},{28,24},{5,1},{9,5},{13... | collective-permute-start | bytes 884744 | tf_op jit(solution)/shard_map/ppermute | solution.py:14
  42.6 8.7 %collective-permute-done.4 = f32[128,576]{0,1:T(8,128)S(1)} collective-permute-done((f32[128,576]{0,1:T(8,128)S(1)}, f32[128,576]{0,1:T(8,128)S(1)}, u32[]{:S(2)}, u32[]{:S(2)}) %collective-permute-start.4) | collective-permute-done | bytes 294944 | tf_op jit(solution)/shard_map/ppermute | solution.py:14
  51.3 0.1 slice_add_fusion.3
  51.3 1.3 %collective-permute-start.5 = (f32[128,576]{0,1:T(8,128)S(1)}, f32[128,576]{0,1:T(8,128)S(1)}, u32[]{:S(2)}, u32[]{:S(2)}) collective-permute-start(f32[128,576]{0,1:T(8,128)S(1)} %slice_add_fusion.3), channel_id=1, source_target_pairs={{4,0},{8,4},{12,8},{16,12},{20,16},{24,20},{28,24},{5,1},{9,5},{13... | collective-permute-start | bytes 884744 | tf_op jit(solution)/shard_map/ppermute | solution.py:14
  52.6 9.5 %collective-permute-done.5 = f32[128,576]{0,1:T(8,128)S(1)} collective-permute-done((f32[128,576]{0,1:T(8,128)S(1)}, f32[128,576]{0,1:T(8,128)S(1)}, u32[]{:S(2)}, u32[]{:S(2)}) %collective-permute-start.5) | collective-permute-done | bytes 294944 | tf_op jit(solution)/shard_map/ppermute | solution.py:14
  62.1 1.3 %collective-permute-start.6 = (f32[128,576]{0,1:T(8,128)S(1)}, f32[128,576]{0,1:T(8,128)S(1)}, u32[]{:S(2)}, u32[]{:S(2)}) collective-permute-start(f32[128,576]{0,1:T(8,128)S(1)} %slice_add_fusion.2), channel_id=1, source_target_pairs={{4,0},{8,4},{12,8},{16,12},{20,16},{24,20},{28,24},{5,1},{9,5},{13... | collective-permute-start | bytes 884744 | tf_op jit(solution)/shard_map/ppermute | solution.py:14
  63.4 11.0 %collective-permute-done.6 = f32[128,576]{0,1:T(8,128)S(1)} collective-permute-done((f32[128,576]{0,1:T(8,128)S(1)}, f32[128,576]{0,1:T(8,128)S(1)}, u32[]{:S(2)}, u32[]{:S(2)}) %collective-permute-start.6) | collective-permute-done | bytes 294944 | tf_op jit(solution)/shard_map/ppermute | solution.py:14
  74.4 1.3 %collective-permute-start.7 = (f32[128,576]{0,1:T(8,128)S(1)}, f32[128,576]{0,1:T(8,128)S(1)}, u32[]{:S(2)}, u32[]{:S(2)}) collective-permute-start(f32[128,576]{0,1:T(8,128)S(1)} %slice_add_fusion.1), channel_id=1, source_target_pairs={{4,0},{8,4},{12,8},{16,12},{20,16},{24,20},{28,24},{5,1},{9,5},{13... | collective-permute-start | bytes 884744 | tf_op jit(solution)/shard_map/ppermute | solution.py:14
  75.7 8.7 %collective-permute-done.7 = f32[128,576]{0,1:T(8,128)S(1)} collective-permute-done((f32[128,576]{0,1:T(8,128)S(1)}, f32[128,576]{0,1:T(8,128)S(1)}, u32[]{:S(2)}, u32[]{:S(2)}) %collective-permute-start.7) | collective-permute-done | bytes 294944 | tf_op jit(solution)/shard_map/ppermute | solution.py:14
  84.5 0.9 copy.17
  85.4 0.0 reduce-scatter.4.cloned.1.call-update
  85.4 0.6 convolution_multiply_fusion.1
  86.0 0.4 copy.14
  86.4 0.4 reshape.45
  86.8 1.5 %copy.15 = f32[128,4,576]{0,2,1:T(8,128)} copy(f32[128,4,576]{2,1,0:T(4,128)S(1)} %reshape.45) | data formatting | bytes 2359296
  88.3 19.4 %reduce-scatter.4.cloned.1.call-done = f32[32,576]{1,0:T(8,128)} async-done(((f32[128,576]{1,0:T(8,128)}), f32[32,576]{1,0:T(8,128)}) %reduce-scatter.4.cloned.1.call-update) | async-done | bytes 73744
  (12 shorter events, 0.3 us)
Async XLA Ops:
  7.2 27.7 %copy-start = (bf16[128,4,512]{2,1,0:T(4,128)(2,1)S(1)}, bf16[128,4,512]{2,1,0:T(4,128)(2,1)}, u32[]{:S(2)}) copy-start(bf16[128,4,512]{2,1,0:T(4,128)(2,1)} %param.7) | copy-start | bytes 1572868
  7.2 28.2 %copy-start.3 = (s32[128]{0:T(128)S(1)}, s32[128]{0:T(128)}, u32[]{:S(2)}) copy-start(s32[128]{0:T(128)} %param.9) | copy-start | bytes 1540
  7.2 28.3 %copy-start.1 = (bf16[128,4,576]{0,2,1:T(8,128)(2,1)S(1)}, bf16[128,4,576]{0,2,1:T(8,128)(2,1)}, u32[]{:S(2)}) copy-start(bf16[128,4,576]{0,2,1:T(8,128)(2,1)} %param.5) | copy-start | bytes 1769476
  7.2 100.5 %reduce-scatter.4.cloned.1.call-start = ((), (), s32[]{:S(2)}) async-start(), calls=%async_computation.1 | async-start | bytes 409600
  7.2 8.4 %collective-permute-start = (bf16[128,576]{0,1:T(8,128)(2,1)}, bf16[128,576]{0,1:T(8,128)(2,1)S(1)}, u32[]{:S(2)}, u32[]{:S(2)}) collective-permute-start(bf16[128,576]{0,1:T(8,128)(2,1)} %param.6), channel_id=1, source_target_pairs={{0,4},{4,8},{8,12},{12,16},{16,20},{20,24},{24,28},{1,5},{5,9},{9,... | collective-permute-start | bytes 442376 | tf_op jit(solution)/shard_map/ppermute | solution.py:14
  15.7 6.9 %collective-permute-start.1 = (bf16[128,576]{0,1:T(8,128)(2,1)S(1)}, bf16[128,576]{0,1:T(8,128)(2,1)S(1)}, u32[]{:S(2)}, u32[]{:S(2)}) collective-permute-start(bf16[128,576]{0,1:T(8,128)(2,1)S(1)} %collective-permute-done), channel_id=1, source_target_pairs={{0,4},{4,8},{8,12},{12,16},{16,20},{20,24},{24,28},{1,5},{5,9},{9,... | collective-permute-start | bytes 442376 | tf_op jit(solution)/shard_map/ppermute | solution.py:14
  22.6 7.0 %collective-permute-start.2 = (bf16[128,576]{0,1:T(8,128)(2,1)S(1)}, bf16[128,576]{0,1:T(8,128)(2,1)S(1)}, u32[]{:S(2)}, u32[]{:S(2)}) collective-permute-start(bf16[128,576]{0,1:T(8,128)(2,1)S(1)} %collective-permute-done.1), channel_id=1, source_target_pairs={{0,4},{4,8},{8,12},{12,16},{16,20},{20,24},{24,28},{1,5},{5,9},{9,... | collective-permute-start | bytes 442376 | tf_op jit(solution)/shard_map/ppermute | solution.py:14
  29.6 7.9 %collective-permute-start.3 = (bf16[128,576]{0,1:T(8,128)(2,1)S(1)}, bf16[128,576]{0,1:T(8,128)(2,1)S(1)}, u32[]{:S(2)}, u32[]{:S(2)}) collective-permute-start(bf16[128,576]{0,1:T(8,128)(2,1)S(1)} %collective-permute-done.2), channel_id=1, source_target_pairs={{0,4},{4,8},{8,12},{12,16},{16,20},{20,24},{24,28},{1,5},{5,9},{9,... | collective-permute-start | bytes 442376 | tf_op jit(solution)/shard_map/ppermute | solution.py:14
  36.3 1.4 %copy-start.2 = (bf16[128,576]{0,1:T(8,128)(2,1)S(1)}, bf16[128,576]{0,1:T(8,128)(2,1)}, u32[]{:S(2)}) copy-start(bf16[128,576]{0,1:T(8,128)(2,1)} %param.6) | copy-start | bytes 442372
  41.3 10.0 %collective-permute-start.4 = (f32[128,576]{0,1:T(8,128)S(1)}, f32[128,576]{0,1:T(8,128)S(1)}, u32[]{:S(2)}, u32[]{:S(2)}) collective-permute-start(f32[128,576]{0,1:T(8,128)S(1)} %slice.30), channel_id=1, source_target_pairs={{4,0},{8,4},{12,8},{16,12},{20,16},{24,20},{28,24},{5,1},{9,5},{13... | collective-permute-start | bytes 884744 | tf_op jit(solution)/shard_map/ppermute | solution.py:14
  51.3 10.8 %collective-permute-start.5 = (f32[128,576]{0,1:T(8,128)S(1)}, f32[128,576]{0,1:T(8,128)S(1)}, u32[]{:S(2)}, u32[]{:S(2)}) collective-permute-start(f32[128,576]{0,1:T(8,128)S(1)} %slice_add_fusion.3), channel_id=1, source_target_pairs={{4,0},{8,4},{12,8},{16,12},{20,16},{24,20},{28,24},{5,1},{9,5},{13... | collective-permute-start | bytes 884744 | tf_op jit(solution)/shard_map/ppermute | solution.py:14
  62.1 12.3 %collective-permute-start.6 = (f32[128,576]{0,1:T(8,128)S(1)}, f32[128,576]{0,1:T(8,128)S(1)}, u32[]{:S(2)}, u32[]{:S(2)}) collective-permute-start(f32[128,576]{0,1:T(8,128)S(1)} %slice_add_fusion.2), channel_id=1, source_target_pairs={{4,0},{8,4},{12,8},{16,12},{20,16},{24,20},{28,24},{5,1},{9,5},{13... | collective-permute-start | bytes 884744 | tf_op jit(solution)/shard_map/ppermute | solution.py:14
  74.4 10.0 %collective-permute-start.7 = (f32[128,576]{0,1:T(8,128)S(1)}, f32[128,576]{0,1:T(8,128)S(1)}, u32[]{:S(2)}, u32[]{:S(2)}) collective-permute-start(f32[128,576]{0,1:T(8,128)S(1)} %slice_add_fusion.1), channel_id=1, source_target_pairs={{4,0},{8,4},{12,8},{16,12},{20,16},{24,20},{28,24},{5,1},{9,5},{13... | collective-permute-start | bytes 884744 | tf_op jit(solution)/shard_map/ppermute | solution.py:14
Sparse Core Ops, SparseCore 0:
  85.5 22.1 reduce-scatter.3
where the time goes:
time: 115 us
  waiting for transfers between devices  65.1 us (57%)
  starting transfers between devices  24.1 us (21%)
  between operations  14.3 us (12%)
  local copies, waits for them, and re-layouts  5.1 us (4%)
  matrix products  3.75 us (3%)
  other arithmetic  2.18 us (2%)
    ppermute x8, waiting for transfers between devices, shifted(): return lax.ppermute(block, axis, route)  45.7 us
    ppermute x8, starting transfers between devices, shifted(): return lax.ppermute(block, axis, route)  24.1 us
    unnamed x2, waiting for transfers between devices  19.4 us
    unnamed x15, local copies, waits for them, and re-layouts  3.32 us
  transfers between devices with their start and end apart: 9, of which 9 were waited for; matrix products, arithmetic and copies ran while one was open for 5% of the time, Pallas kernels for 0%

commit v1 on v0

v1 whole, which is shorter than its diff:
```python
import functools

import jax
import jax.numpy as jnp
from jax import lax
from jax.experimental import pallas as pl
from jax.experimental.pallas import tpu as pltpu
from jax.sharding import PartitionSpec as P

VAL = 512
QK_HEAD = 192
STEPS = 5
MESH = pl.DeviceIdType.MESH
SCALE = QK_HEAD ** (-0.5)
F32 = jnp.float32
BF16 = jnp.bfloat16


def dot(a, b, ca, cb):
    return lax.dot_general(a, b, (((ca,), (cb,)), ((), ())), preferred_element_type=F32)


def fused_kernel(n_seq, n_head, levels,
                 q_hbm, lat_hbm, g_hbm, o_hbm, first_ref,
                 qg_ref, lg_ref,
                 q_v, g_v, o_v, gh_v, win, s_v, dp_v, ds_v, accs, wires, recvs,
                 wire_seq, recv_seq,
                 in_sem, gs_sem, gr_sem, hs_sem, hr_sem, rs_sem, rr_sem):
    heads, width, rows = q_v.shape
    back = STEPS - 1
    part = width // n_head
    s = lax.axis_index("seq")
    h = lax.axis_index("head")
    bits = [(h // (1 << t)) % 2 for t in range(levels)]
    partners = [h + (1 << t) * (1 - 2 * bits[t]) for t in range(levels)]

    loads = [
        pltpu.make_async_copy(lat_hbm, win.at[0], in_sem.at[0]),
        pltpu.make_async_copy(q_hbm, q_v, in_sem.at[1]),
        pltpu.make_async_copy(g_hbm, g_v, in_sem.at[2]),
        pltpu.make_async_copy(o_hbm, o_v, in_sem.at[3]),
    ]
    for copy in loads:
        copy.start()

    barrier = pltpu.get_barrier_semaphore()

    def greet(dev):
        pl.semaphore_signal(barrier, inc=1, device_id=dev, device_id_type=MESH)

    for t in range(levels):
        greet((s, partners[t]))
    for k in range(1, STEPS):
        @pl.when(s >= k)
        def _():
            greet((s - k, h))

        @pl.when(s + k < n_seq)
        def _():
            greet((s + k, h))
    peers = levels
    for k in range(1, min(STEPS, n_seq)):
        peers = peers + lax.div(s - k + n_seq, n_seq) + lax.div(2 * n_seq - 1 - s - k, n_seq)
    pl.semaphore_wait(barrier, peers)

    def chunk(q):
        return pl.ds(pl.multiple_of(q * part, 16), part)

    def seq_send(k):
        return pltpu.make_async_remote_copy(
            src_ref=lat_hbm.at[chunk(h)], dst_ref=win.at[k, chunk(h)],
            send_sem=gs_sem.at[k - 1, 0], recv_sem=gr_sem.at[k - 1, 0],
            device_id=(s + k, h), device_id_type=MESH)

    for k in range(1, STEPS):
        @pl.when(s + k < n_seq)
        def _():
            seq_send(k).start()

    plan = []
    slot = 1
    for t in range(levels - 1, -1, -1):
        low = 1 << (t + 1)
        stage = []
        for m in range(n_head // low):
            stage.append((slot, h % low + low * m))
            slot += 1
        plan.append((t, stage))

    def pass_on(k, t, sl, q):
        return pltpu.make_async_remote_copy(
            src_ref=win.at[k, chunk(q)], dst_ref=win.at[k, chunk(q)],
            send_sem=gs_sem.at[k - 1, sl], recv_sem=gr_sem.at[k - 1, sl],
            device_id=(s, partners[t]), device_id_type=MESH)

    for k in range(1, STEPS):
        @pl.when(s < k)
        def _():
            win[k] = jnp.zeros((width, rows), BF16)

    first = first_ref[...]
    query_pos = s * rows + lax.broadcasted_iota(jnp.int32, (1, rows), 1)

    def score_block(k):
        keys = win[k].T
        key_pos = (s - k) * rows + lax.broadcasted_iota(jnp.int32, (rows, rows), 0)
        visible = (key_pos >= first) & (key_pos <= query_pos)
        best = []
        for hd in range(heads):
            cols = pl.ds(hd * rows, rows)
            sc = dot(keys, q_v[hd], 1, 0) * SCALE
            sc = jnp.where(visible, sc, -1e30)
            s_v[k, :, cols] = sc
            best.append(jnp.max(sc, axis=0, keepdims=True))
        dp_v[k] = dot(keys[:, :VAL], gh_v[...], 1, 1)
        return jnp.concatenate(best, axis=1)

    for copy in loads[1:]:
        copy.wait()
    dots = []
    for hd in range(heads):
        g_h = g_v[:, hd, :]
        gh_v[pl.ds(hd * rows, rows), :] = g_h
        prod = jnp.sum(g_h.astype(F32) * o_v[:, hd, :].astype(F32), axis=1, keepdims=True)
        dots.append(jnp.broadcast_to(prod, (rows, rows)).T[0:1, :])
    row_dot = jnp.concatenate(dots, axis=1)
    loads[0].wait()
    row_max = score_block(0)

    for level in range(len(plan) + 1):
        for k in range(1, STEPS):
            @pl.when(s >= k)
            def _():
                if level == 0:
                    seq_send(k).wait_recv()
                else:
                    t, stage = plan[level - 1]
                    for sl, q in stage:
                        pass_on(k, t, sl, q).wait_recv()
                if level < len(plan):
                    t, stage = plan[level]
                    for sl, q in stage:
                        pass_on(k, t, sl, q).start()
            if level == len(plan):
                row_max = jnp.maximum(row_max, score_block(k))

    total = jnp.zeros_like(row_max)
    for k in range(STEPS):
        total += jnp.sum(jnp.exp(s_v[k] - row_max), axis=0, keepdims=True)
    log_norm = row_max + jnp.log(total)

    grads = gh_v[...]
    queries = jnp.concatenate([q_v[hd] for hd in range(heads)], axis=1)

    def head_copy(t, k, m):
        src = 2 * m + 1 - bits[t]
        return pltpu.make_async_remote_copy(
            src_ref=wires[t].at[k, src], dst_ref=recvs[t].at[k, m],
            send_sem=hs_sem[t].at[k, m], recv_sem=hr_sem[t].at[k, m],
            device_id=(s, partners[t]), device_id_type=MESH)

    def kept(t):
        return n_head >> (t + 1)

    order = list(range(back, -1, -1))
    for k in order:
        probs = jnp.exp(s_v[k] - log_norm)
        score_grad = (probs * (dp_v[k] - row_dot)).astype(BF16)
        ds_v[pl.ds(k * rows, rows), :] = score_grad
        lat = dot(score_grad, queries, 1, 1) * SCALE
        val = dot(probs.astype(BF16), grads, 1, 0)
        lat = jnp.concatenate([lat[:, :VAL] + val, lat[:, VAL:]], axis=1)
        lat = lat.reshape(n_head, rows // n_head, width)
        accs[0][k] = lat
        wires[0][k] = lat.astype(BF16)
        for m in range(kept(0)):
            head_copy(0, k, m).start()

    def seq_copy(k):
        return pltpu.make_async_remote_copy(
            src_ref=wire_seq.at[k - 1], dst_ref=recv_seq.at[k - 1],
            send_sem=rs_sem.at[k - 1], recv_sem=rr_sem.at[k - 1],
            device_id=(s - k, h), device_id_type=MESH)

    window = jnp.concatenate([win[k] for k in range(STEPS)], axis=1)

    def query_grad(hd):
        qg_ref[hd] = dot(window, ds_v[:, pl.ds(hd * rows, rows)], 1, 0) * SCALE

    done = 0
    for t in range(levels):
        if done < heads:
            query_grad(done)
            done += 1
        for k in order:
            for m in range(kept(t)):
                head_copy(t, k, m).wait_recv()
                new = accs[t][k, 2 * m + bits[t]] + recvs[t][k, m].astype(F32)
                accs[t + 1][k, m] = new
                if t + 1 < levels:
                    wires[t + 1][k, m] = new.astype(BF16)
                elif k:
                    wire_seq[k - 1] = new.astype(BF16)
            if t + 1 < levels:
                for m in range(kept(t + 1)):
                    head_copy(t + 1, k, m).start()
            elif k:
                @pl.when(s >= k)
                def _():
                    seq_copy(k).start()
    while done < heads:
        query_grad(done)
        done += 1

    lg_ref[...] = accs[levels][0, 0]
    for k in range(1, STEPS):
        @pl.when(s + k < n_seq)
        def _():
            seq_copy(k).wait_recv()
            lg_ref[...] += recv_seq[k - 1].astype(F32)

    for k in range(1, STEPS):
        @pl.when(s + k < n_seq)
        def _():
            seq_send(k).wait_send()

        @pl.when(s >= k)
        def _():
            for t, stage in plan:
                for sl, q in stage:
                    pass_on(k, t, sl, q).wait_send()
            seq_copy(k).wait_send()
    for t in range(levels):
        for k in order:
            for m in range(kept(t)):
                head_copy(t, k, m).wait_send()


def fused_body(n_seq, n_head, query, latents, out_grad, saved_out, first_key):
    rows, heads, width = query.shape
    levels = n_head.bit_length() - 1
    piece = rows // n_head
    cells = rows * heads
    hbm = pl.BlockSpec(memory_space=pltpu.MemorySpace.HBM)
    vmem = pl.BlockSpec(memory_space=pltpu.VMEM)
    dma = pltpu.SemaphoreType.DMA
    scratch = [
        pltpu.VMEM((heads, width, rows), BF16),
        pltpu.VMEM((rows, heads, VAL), BF16),
        pltpu.VMEM((rows, heads, VAL), BF16),
        pltpu.VMEM((cells, VAL), BF16),
        pltpu.VMEM((STEPS, width, rows), BF16),
        pltpu.VMEM((STEPS, rows, cells), F32),
        pltpu.VMEM((STEPS, rows, cells), F32),
        pltpu.VMEM((STEPS * rows, cells), BF16),
        [pltpu.VMEM((STEPS, n_head >> t, piece, width), F32) for t in range(levels + 1)],
        [pltpu.VMEM((STEPS, n_head >> t, piece, width), BF16) for t in range(levels)],
        [pltpu.VMEM((STEPS, n_head >> (t + 1), piece, width), BF16) for t in range(levels)],
        pltpu.VMEM((STEPS - 1, piece, width), BF16),
        pltpu.VMEM((STEPS - 1, piece, width), BF16),
        dma((4,)),
        dma((STEPS - 1, n_head)),
        dma((STEPS - 1, n_head)),
        [dma((STEPS, n_head >> (t + 1))) for t in range(levels)],
        [dma((STEPS, n_head >> (t + 1))) for t in range(levels)],
        dma((STEPS - 1,)),
        dma((STEPS - 1,)),
    ]
    query_grad, latent_grad = pl.pallas_call(
        functools.partial(fused_kernel, n_seq, n_head, levels),
        out_shape=(
            jax.ShapeDtypeStruct((heads, width, rows), F32),
            jax.ShapeDtypeStruct((piece, width), F32),
        ),
        in_specs=[hbm, hbm, hbm, hbm, vmem],
        out_specs=(vmem, vmem),
        scratch_shapes=scratch,
        compiler_params=pltpu.CompilerParams(
            collective_id=0, has_side_effects=True, vmem_limit_bytes=48 * 1024 * 1024
        ),
    )(
        jnp.transpose(query, (1, 2, 0)),
        latents.T,
        out_grad,
        saved_out,
        first_key.reshape(1, rows),
    )
    return jnp.transpose(query_grad, (2, 0, 1)), latent_grad


def shifted(block, axis, distance):
    devices = range(lax.axis_size(axis))
    route = [(i - distance, i) for i in devices if i - distance in devices]
    return lax.ppermute(block, axis, route)


def visibility(first, query_start, key_start, rows, heads, keys):
    query_pos = jnp.repeat(query_start + jnp.arange(rows, dtype=jnp.int32), heads)
    first_rows = jnp.repeat(first, heads)
    key_pos = key_start + jnp.arange(keys, dtype=jnp.int32)
    return (key_pos[None, :] >= first_rows[:, None]) & (key_pos[None, :] <= query_pos[:, None])


def attention_grads(queries, window, grads_out, outputs, visible):
    scores = jnp.dot(queries, window.T, preferred_element_type=F32) * SCALE
    scores = jnp.where(visible, scores, -1e30)
    row_max = jnp.max(scores, axis=1, keepdims=True)
    row_total = jnp.sum(jnp.where(visible, jnp.exp(scores - row_max), 0.0), axis=1, keepdims=True)
    log_norm = row_max + jnp.log(row_total)
    probs = jnp.where(visible, jnp.exp(scores - log_norm), 0.0)
    row_dot = jnp.sum(grads_out.astype(F32) * outputs.astype(F32), axis=1, keepdims=True)
    prob_grad = jnp.dot(grads_out, window[:, :VAL].T, preferred_element_type=F32)
    score_grad = (probs * (prob_grad - row_dot)).astype(BF16)
    query_grad = jnp.dot(score_grad, window, preferred_element_type=F32) * SCALE
    latent_grad = dot(score_grad, queries, 0, 0) * SCALE
    value_grad = dot(probs.astype(BF16), grads_out, 0, 0)
    padding = jnp.zeros((window.shape[0], window.shape[1] - VAL), F32)
    return query_grad, latent_grad + jnp.concatenate([value_grad, padding], axis=1)


def plain_body(query, latents, out_grad, saved_out, first_key):
    rows, heads, width = query.shape
    here = lax.axis_index("seq")
    blocks = [latents]
    for _ in range(STEPS - 1):
        blocks.append(shifted(blocks[-1], "seq", 1))
    window = jnp.concatenate(blocks[::-1], axis=0)
    start = here * rows
    visible = visibility(
        first_key, start, start - (STEPS - 1) * rows, rows, heads, STEPS * rows
    )
    query_grad, latent_grad = attention_grads(
        query.reshape(rows * heads, width),
        window,
        out_grad.reshape(rows * heads, VAL),
        saved_out.reshape(rows * heads, VAL),
        visible,
    )
    pieces = latent_grad.reshape(STEPS, rows, width)
    carried = pieces[0]
    for hop in range(1, STEPS):
        carried = shifted(carried, "seq", -1) + pieces[hop]
    carried = lax.psum_scatter(carried, "head", scatter_dimension=0, tiled=True)
    return query_grad.reshape(rows, heads, width), carried


def solution(mesh):
    n_seq, n_head = mesh.shape["seq"], mesh.shape["head"]

    def body(query, latents, out_grad, saved_out, first_key):
        rows, heads, width = query.shape
        fits = n_head & (n_head - 1) == 0 and n_head > 1
        fits = fits and rows % (16 * n_head) == 0 and width % (16 * n_head) == 0
        if fits:
            return fused_body(n_seq, n_head, query, latents, out_grad, saved_out, first_key)
        return plain_body(query, latents, out_grad, saved_out, first_key)

    in_specs = (
        P("seq", "head", None),
        P("seq", None),
        P("seq", "head", None),
        P("seq", "head", None),
        P("seq"),
    )
    out_specs = (P("seq", "head", None), P(("seq", "head"), None))
    return jax.shard_map(body, mesh=mesh, in_specs=in_specs, out_specs=out_specs, check_vma=False)
```

time: 115 us -> 35.2 us (0.31)
  the two profiles are of different devices: /device:TPU:0 before, /device:TPU:14 now
where the time goes in v1:
time: 35.2 us; the launch traced here: 34.9 us
  Pallas kernels  27.9 us (79%)
  local copies, waits for them, and re-layouts  6.35 us (18%)
  between operations  0.65 us (2%)
    pallas_call x1, Pallas kernels, fused_body(): pl.pallas_call(functools.partial(fused_kernel, n_seq, n_head, levels), ou...  27.9 us
    unnamed x12, local copies, waits for them, and re-layouts  6.35 us

profile of v1, /device:TPU:14, one launch (start us, length us, event | category | flops | bytes accessed | tf_op | source)
XLA Modules:
  0.0 34.9 jit_solution(11363167558013879441)
XLA Ops:
  0.6 0.0 copy-start
  0.6 1.1 %copy-done = bf16[128,4,576]{0,2,1:T(8,128)(2,1)S(1)} copy-done((bf16[128,4,576]{0,2,1:T(8,128)(2,1)S(1)}, bf16[128,4,576]{0,2,1:T(8,128)(2,1)}, u32[]{:S(2)}) %copy-start) | copy-done | bytes 589848
  1.7 0.0 copy-start.1
  1.7 1.0 %copy-done.1 = bf16[128,4,512]{2,1,0:T(4,128)(2,1)S(1)} copy-done((bf16[128,4,512]{2,1,0:T(4,128)(2,1)S(1)}, bf16[128,4,512]{2,1,0:T(4,128)(2,1)}, u32[]{:S(2)}) %copy-start.1) | copy-done | bytes 524312
  2.7 0.0 copy-start.2
  2.7 1.0 %copy-done.2 = bf16[128,4,512]{2,1,0:T(4,128)(2,1)S(1)} copy-done((bf16[128,4,512]{2,1,0:T(4,128)(2,1)S(1)}, bf16[128,4,512]{2,1,0:T(4,128)(2,1)}, u32[]{:S(2)}) %copy-start.2) | copy-done | bytes 524312
  3.8 0.0 copy-start.3
  3.8 0.9 %copy-done.3 = bf16[128,576]{0,1:T(8,128)(2,1)S(1)} copy-done((bf16[128,576]{0,1:T(8,128)(2,1)S(1)}, bf16[128,576]{0,1:T(8,128)(2,1)}, u32[]{:S(2)}) %copy-start.3) | copy-done | bytes 147480
  4.7 0.0 copy-start.4
  4.7 0.7 %copy-done.4 = s32[128]{0:T(128)S(1)} copy-done((s32[128]{0:T(128)S(1)}, s32[128]{0:T(128)}, u32[]{:S(2)}) %copy-start.4) | copy-done | bytes 536
  5.3 27.9 %shard_map.68 = (f32[4,576,128]{2,1,0:T(8,128)S(1)}, f32[32,576]{1,0:T(8,128)S(1)}) custom-call(bf16[4,576,128]{2,1,0:T(8,128)(2,1)S(1)} %bitcast.5, bf16[576,128]{1,0:T(8,128)(2,1)S(1)} %bitcast.6, bf16[128,4,512]{2,1,0:T(4,128)(2,1)S(1)} %copy-done.1, bf16[128,4,512]{2,1,0:T(4,128)(2,1)S(1)} %copy-done.2, s32[1,128]{1,0:T(1,128)S(1)} %bitcast.7), custom_call_target="tpu_custom_call" | custom-call | tf_op jit(solution)/shard_map/pallas_call | solution.py:269
  33.3 1.0 %copy.9 = f32[128,4,576]{0,2,1:T(8,128)} copy(f32[128,4,576]{0,2,1:T(8,128)S(1)} %bitcast.4) | data formatting | bytes 2359296
  34.3 0.6 %copy.10 = f32[32,576]{1,0:T(8,128)} copy(f32[32,576]{1,0:T(8,128)S(1)} %get-tuple-element.9) | data formatting | bytes 147456
Async XLA Ops:
  0.6 1.1 %copy-start = (bf16[128,4,576]{0,2,1:T(8,128)(2,1)S(1)}, bf16[128,4,576]{0,2,1:T(8,128)(2,1)}, u32[]{:S(2)}) copy-start(bf16[128,4,576]{0,2,1:T(8,128)(2,1)} %param.5) | copy-start | bytes 1769476
  1.7 1.0 %copy-start.1 = (bf16[128,4,512]{2,1,0:T(4,128)(2,1)S(1)}, bf16[128,4,512]{2,1,0:T(4,128)(2,1)}, u32[]{:S(2)}) copy-start(bf16[128,4,512]{2,1,0:T(4,128)(2,1)} %g_hbm.1) | copy-start | bytes 1572868
  2.7 1.0 %copy-start.2 = (bf16[128,4,512]{2,1,0:T(4,128)(2,1)S(1)}, bf16[128,4,512]{2,1,0:T(4,128)(2,1)}, u32[]{:S(2)}) copy-start(bf16[128,4,512]{2,1,0:T(4,128)(2,1)} %o_hbm.1) | copy-start | bytes 1572868
  3.8 0.9 %copy-start.3 = (bf16[128,576]{0,1:T(8,128)(2,1)S(1)}, bf16[128,576]{0,1:T(8,128)(2,1)}, u32[]{:S(2)}) copy-start(bf16[128,576]{0,1:T(8,128)(2,1)} %param.6) | copy-start | bytes 442372
  4.7 0.7 %copy-start.4 = (s32[128]{0:T(128)S(1)}, s32[128]{0:T(128)}, u32[]{:S(2)}) copy-start(s32[128]{0:T(128)} %param.9) | copy-start | bytes 1540

commit v2 on v1

--- a/solution.py
+++ b/solution.py
@@ -21,9 +21,9 @@
 
 
 def fused_kernel(n_seq, n_head, levels,
-                 q_hbm, lat_hbm, g_hbm, o_hbm, first_ref,
+                 q_hbm, lat_hbm, g_hbm, o_hbm, first_hbm,
                  qg_ref, lg_ref,
-                 q_v, g_v, o_v, gh_v, win, s_v, dp_v, ds_v, accs, wires, recvs,
+                 q_v, g_v, o_v, first_v, gh_v, win, s_v, dp_v, ds_v, accs, wires, recvs,
                  wire_seq, recv_seq,
                  in_sem, gs_sem, gr_sem, hs_sem, hr_sem, rs_sem, rr_sem):
     heads, width, rows = q_v.shape
@@ -39,6 +39,7 @@
         pltpu.make_async_copy(q_hbm, q_v, in_sem.at[1]),
         pltpu.make_async_copy(g_hbm, g_v, in_sem.at[2]),
         pltpu.make_async_copy(o_hbm, o_v, in_sem.at[3]),
+        pltpu.make_async_copy(first_hbm, first_v, in_sem.at[4]),
     ]
     for copy in loads:
         copy.start()
@@ -98,7 +99,6 @@
         def _():
             win[k] = jnp.zeros((width, rows), BF16)
 
-    first = first_ref[...]
     query_pos = s * rows + lax.broadcasted_iota(jnp.int32, (1, rows), 1)
 
     def score_block(k):
@@ -117,6 +117,7 @@
 
     for copy in loads[1:]:
         copy.wait()
+    first = first_v[...]
     dots = []
     for hd in range(heads):
         g_h = g_v[:, hd, :]
@@ -127,22 +128,23 @@
     loads[0].wait()
     row_max = score_block(0)
 
-    for level in range(len(plan) + 1):
-        for k in range(1, STEPS):
-            @pl.when(s >= k)
-            def _():
-                if level == 0:
-                    seq_send(k).wait_recv()
-                else:
-                    t, stage = plan[level - 1]
-                    for sl, q in stage:
-                        pass_on(k, t, sl, q).wait_recv()
-                if level < len(plan):
-                    t, stage = plan[level]
-                    for sl, q in stage:
-                        pass_on(k, t, sl, q).start()
-            if level == len(plan):
-                row_max = jnp.maximum(row_max, score_block(k))
+    arrivals = [(k + 1.5 * level, level, k)
+                for level in range(len(plan) + 1) for k in range(1, STEPS)]
+    for _, level, k in sorted(arrivals):
+        @pl.when(s >= k)
+        def _():
+            if level == 0:
+                seq_send(k).wait_recv()
+            else:
+                t, stage = plan[level - 1]
+                for sl, q in stage:
+                    pass_on(k, t, sl, q).wait_recv()
+            if level < len(plan):
+                t, stage = plan[level]
+                for sl, q in stage:
+                    pass_on(k, t, sl, q).start()
+        if level == len(plan):
+            row_max = jnp.maximum(row_max, score_block(k))
 
     total = jnp.zeros_like(row_max)
     for k in range(STEPS):
@@ -163,7 +165,8 @@
         return n_head >> (t + 1)
 
     order = list(range(back, -1, -1))
-    for k in order:
+
+    def latent_grad(k):
         probs = jnp.exp(s_v[k] - log_norm)
         score_grad = (probs * (dp_v[k] - row_dot)).astype(BF16)
         ds_v[pl.ds(k * rows, rows), :] = score_grad
@@ -187,30 +190,27 @@
     def query_grad(hd):
         qg_ref[hd] = dot(window, ds_v[:, pl.ds(hd * rows, rows)], 1, 0) * SCALE
 
-    done = 0
+    def halve(t, k):
+        for m in range(kept(t)):
+            head_copy(t, k, m).wait_recv()
+            new = accs[t][k, 2 * m + bits[t]] + recvs[t][k, m].astype(F32)
+            accs[t + 1][k, m] = new
+            if t + 1 < levels:
+                wires[t + 1][k, m] = new.astype(BF16)
+                head_copy(t + 1, k, m // 2).start() if m % 2 else None
+            elif k:
+                wire_seq[k - 1] = new.astype(BF16)
+        if t + 1 == levels and k:
+            @pl.when(s >= k)
+            def _():
+                seq_copy(k).start()
+
+    work = [(i, 0, latent_grad, (k,)) for i, k in enumerate(order)]
     for t in range(levels):
-        if done < heads:
-            query_grad(done)
-            done += 1
-        for k in order:
-            for m in range(kept(t)):
-                head_copy(t, k, m).wait_recv()
-                new = accs[t][k, 2 * m + bits[t]] + recvs[t][k, m].astype(F32)
-                accs[t + 1][k, m] = new
-                if t + 1 < levels:
-                    wires[t + 1][k, m] = new.astype(BF16)
-                elif k:
-                    wire_seq[k - 1] = new.astype(BF16)
-            if t + 1 < levels:
-                for m in range(kept(t + 1)):
-                    head_copy(t + 1, k, m).start()
-            elif k:
-                @pl.when(s >= k)
-                def _():
-                    seq_copy(k).start()
-    while done < heads:
-        query_grad(done)
-        done += 1
+        work += [(i + 3.5 + 5 * t, 2, halve, (t, k)) for i, k in enumerate(order)]
+    work += [(len(order) + 2.5 + i, 1, query_grad, (i,)) for i in range(heads)]
+    for _, _, step, operands in sorted(work, key=lambda item: item[:2]):
+        step(*operands)
 
     lg_ref[...] = accs[levels][0, 0]
     for k in range(1, STEPS):
@@ -248,6 +248,7 @@
         pltpu.VMEM((heads, width, rows), BF16),
         pltpu.VMEM((rows, heads, VAL), BF16),
         pltpu.VMEM((rows, heads, VAL), BF16),
+        pltpu.VMEM((1, rows), jnp.int32),
         pltpu.VMEM((cells, VAL), BF16),
         pltpu.VMEM((STEPS, width, rows), BF16),
         pltpu.VMEM((STEPS, rows, cells), F32),
@@ -258,7 +259,7 @@
         [pltpu.VMEM((STEPS, n_head >> (t + 1), piece, width), BF16) for t in range(levels)],
         pltpu.VMEM((STEPS - 1, piece, width), BF16),
         pltpu.VMEM((STEPS - 1, piece, width), BF16),
-        dma((4,)),
+        dma((5,)),
         dma((STEPS - 1, n_head)),
         dma((STEPS - 1, n_head)),
         [dma((STEPS, n_head >> (t + 1))) for t in range(levels)],
@@ -272,18 +273,23 @@
             jax.ShapeDtypeStruct((heads, width, rows), F32),
             jax.ShapeDtypeStruct((piece, width), F32),
         ),
-        in_specs=[hbm, hbm, hbm, hbm, vmem],
+        in_specs=[hbm] * 5,
         out_specs=(vmem, vmem),
         scratch_shapes=scratch,
         compiler_params=pltpu.CompilerParams(
-            collective_id=0, has_side_effects=True, vmem_limit_bytes=48 * 1024 * 1024
+            collective_id=0, has_side_effects=True, vmem_limit_bytes=40 * 1024 * 1024
         ),
     )(
-        jnp.transpose(query, (1, 2, 0)),
-        latents.T,
-        out_grad,
-        saved_out,
-        first_key.reshape(1, rows),
+        *(
+            pltpu.with_memory_space_constraint(x, pltpu.MemorySpace.HBM)
+            for x in (
+                jnp.transpose(query, (1, 2, 0)),
+                latents.T,
+                out_grad,
+                saved_out,
+                first_key.reshape(1, rows),
+            )
+        ),
     )
     return jnp.transpose(query_grad, (2, 0, 1)), latent_grad
 

time: 35.2 us -> 31 us (0.88)
  the two profiles are of different devices: /device:TPU:14 before, /device:TPU:0 now
where the time goes in v2:
time: 31 us; the launch traced here: 30.9 us
  Pallas kernels  28.6 us (92%)
  local copies, waits for them, and re-layouts  1.65 us (5%)
  between operations  0.64 us (2%)
    pallas_call x1, Pallas kernels, fused_body(): pl.pallas_call(functools.partial(fused_kernel, n_seq, n_head, levels), ou...  28.6 us
    unnamed x2, local copies, waits for them, and re-layouts  1.65 us

profile of v2, /device:TPU:0, one launch (start us, length us, event | category | flops | bytes accessed | tf_op | source)
XLA Modules:
  0.0 30.9 jit_solution(459977117023837569)
XLA Ops:
  0.6 28.6 %shard_map.68 = (f32[4,576,128]{2,1,0:T(8,128)S(1)}, f32[32,576]{1,0:T(8,128)S(1)}) custom-call(bf16[4,576,128]{2,1,0:T(8,128)(2,1)} %bitcast.5, bf16[576,128]{1,0:T(8,128)(2,1)} %bitcast.6, bf16[128,4,512]{2,1,0:T(4,128)(2,1)} %g_hbm.1, bf16[128,4,512]{2,1,0:T(4,128)(2,1)} %o_hbm.1, s32[1,128]{1,0:T(1,128)} %bitcast.7), custom_call_target="tpu_custom_call" | custom-call | tf_op jit(solution)/shard_map/pallas_call | solution.py:270
  29.2 1.0 %copy.9 = f32[128,4,576]{0,2,1:T(8,128)} copy(f32[128,4,576]{0,2,1:T(8,128)S(1)} %bitcast.4) | data formatting | bytes 2359296
  30.2 0.6 %copy.10 = f32[32,576]{1,0:T(8,128)} copy(f32[32,576]{1,0:T(8,128)S(1)} %get-tuple-element.9) | data formatting | bytes 147456
